TPU v7x, 128 devices: a whole 4x4x4 slice. The times are simulated.
128 devices in a mesh: row: 8 (over y, z_lo), col: 16 (over x, z_hi, core).
Axes of the slice: x: 4, y: 4, z: 4 (z_hi: 2, z_lo: 2; z = z_hi * 2 + z_lo), core: 2. Of those that a mesh axis runs over, the one named last changes fastest.
Arguments:
- tokens: bfloat16 [4096, 6144], P('row', 'col'), may hold values from -40 to 40
- ln_gain: float32 [6144], replicated, may hold values from 0.25 to 1.75
- w_qkv: bfloat16 [6144, 3, 4096], P('row', None, 'col'), may hold values from -0.078125 to 0.078125
- q_gain: float32 [128], replicated, may hold values from 0.1 to 1.9
- k_gain: float32 [128], replicated, may hold values from 0.1 to 1.9
- w_up: bfloat16 [6144, 12288], P('row', 'col'), may hold values from -0.078125 to 0.078125
- w_out: bfloat16 [4096, 6144], P('col', 'row'), may hold values from -0.5 to 0.5
- w_down: bfloat16 [12288, 6144], P('col', 'row'), may hold values from -0.078125 to 0.078125
Outputs:
- mixed: bfloat16 [4096, 6144], P('row', 'col')
All inputs are finite; a program needn't handle non-finite values.
Results may differ from a plain program's by a relative error of at most 0.017.
Values may be sent and summed in bfloat16 or wider, within the bound.
No kernel may reach another device: no remote copies, remote signals or barrier semaphores. Data moves between devices by JAX's collectives and lax.ppermute only.
A program may use at most 128 MiB of HBM per device.

v0:
```python
import math
import jax
import jax.numpy as jnp
from jax import lax
from jax.sharding import PartitionSpec as P

HD = 128
PATCHES = 256
epsilon = 1e-06


def layer_norm(values_in, gain_vec):
    x_float = values_in.astype(jnp.float32)
    centre = jnp.mean(x_float, axis=-1, keepdims=True)
    deviation = x_float - centre
    variance = jnp.mean(deviation * deviation, axis=-1, keepdims=True)
    return deviation * lax.rsqrt(variance + epsilon) * gain_vec


def attend(projected, q_gain, k_gain):
    tok_count = projected.shape[0]
    frame_count = tok_count // PATCHES
    arranged = projected.reshape(frame_count, PATCHES, 3, -1, HD)
    queries = layer_norm(arranged[:, :, 0], q_gain).astype(jnp.bfloat16)
    key_vecs = layer_norm(arranged[:, :, 1], k_gain).astype(jnp.bfloat16)
    value_vecs = arranged[:, :, 2].astype(jnp.bfloat16)
    scores = jnp.einsum(
        "fqhd,fkhd->fhqk", queries, key_vecs, preferred_element_type=jnp.float32
    ) / math.sqrt(HD)
    exponent = jnp.exp(scores)
    attn_probs = (exponent / jnp.sum(exponent, axis=-1, keepdims=True)).astype(jnp.bfloat16)
    attended = jnp.einsum(
        "fhqk,fkhd->fqhd", attn_probs, value_vecs, preferred_element_type=jnp.float32
    )
    return attended.astype(jnp.bfloat16).reshape(tok_count, -1)


def shards(tokens, ln_gain, w_qkv, q_gain, k_gain, w_up, w_out, w_down):
    gathered = lax.all_gather(tokens, "col", axis=1, tiled=True)
    normed = layer_norm(gathered, ln_gain).astype(jnp.bfloat16)

    def add_rows(weight_rows):
        flattened = weight_rows.reshape(weight_rows.shape[0], -1)
        return jnp.dot(normed, flattened, preferred_element_type=jnp.float32)

    weight_rows = (
        lax.all_gather(w_qkv, "row", axis=0, tiled=True),
        lax.all_gather(w_up, "row", axis=0, tiled=True),
    )
    projected = add_rows(weight_rows[0])
    pre_act = add_rows(weight_rows[1])
    attended = attend(projected, q_gain, k_gain)
    activated = jax.nn.gelu(pre_act, approximate=False).astype(jnp.bfloat16)
    column_block = jnp.dot(
        attended,
        lax.all_gather(w_out, "row", axis=1, tiled=True),
        preferred_element_type=jnp.float32,
    )
    column_block = column_block + jnp.dot(
        activated,
        lax.all_gather(w_down, "row", axis=1, tiled=True),
        preferred_element_type=jnp.float32,
    )
    summed = lax.psum_scatter(
        column_block.astype(jnp.bfloat16), "col", scatter_dimension=1, tiled=True
    ).astype(jnp.float32)
    return (tokens.astype(jnp.float32) + summed).astype(jnp.bfloat16)


def solution(mesh):
    in_specs = (
        P("row", "col"),
        P(),
        P("row", None, "col"),
        P(),
        P(),
        P("row", "col"),
        P("col", "row"),
        P("col", "row"),
    )
    out_specs = P("row", "col")
    return jax.shard_map(shards, mesh=mesh, in_specs=in_specs, out_specs=out_specs, check_vma=False)
```

profile of v0, /device:TPU:0, one launch (start us, length us, event | category | flops | bytes accessed | tf_op | source)
XLA Modules:
  0.0 848.3 jit_solution(13845213418589235404)
XLA Ops:
  6.5 0.0 all-gather.6.cloned.1.call-start
  6.5 0.7 all-gather.6.cloned.1.call-update
  7.3 0.0 all-gather.8.cloned.1.call-start
  7.3 2.4 copy.17
  9.7 0.0 all-gather.8.cloned.1.call-update
  9.7 0.0 all-gather.14.cloned.1.call-start
  9.8 0.7 all-gather.14.cloned.1.call-update
  10.5 0.0 all-gather.12.cloned.1.call-start
  10.5 0.5 all-gather.12.cloned.1.call-update
  11.0 0.0 all-gather.10.cloned.1.call-start
  11.1 0.5 all-gather.10.cloned.1.call-update
  11.6 0.0 reduce-scatter.4.cloned.1.call-start
  11.7 70.0 %all-gather.6.cloned.1.call-done = bf16[512,6144]{1,0:T(8,128)(2,1)} async-done(((bf16[512,384]{1,0:T(8,128)(2,1)}), bf16[512,6144]{1,0:T(8,128)(2,1)}) %all-gather.6.cloned.1.call-update) | async-done | bytes 6291472 | tf_op jit(solution)/shard_map/all_gather | solution.py:39
  81.6 0.0 copy-start
  81.6 3.8 convert_reduce_fusion
  85.5 0.7 copy-done
  86.2 0.0 copy-start.2
  86.2 1.8 fusion.2
  88.0 0.0 copy-done.2
  88.0 6.3 fusion.4
  94.3 175.4 %all-gather.8.cloned.1.call-done = bf16[6144,3,256]{0,2,1:T(8,128)(2,1)} async-done(((bf16[768,3,256]{0,2,1:T(8,128)(2,1)}), bf16[6144,3,256]{0,2,1:T(8,128)(2,1)}) %all-gather.8.cloned.1.call-update) | async-done | bytes 9437200 | tf_op jit(solution)/shard_map/all_gather | solution.py:47
  269.8 9.5 %fusion.93 = f32[2,256,3,2,128]{1,4,3,2,0:T(8,128)S(1)} fusion(bf16[2,256,6144,1,1]{2,1,4,3,0:T(8,128)(2,1)} %bitcast.46, bf16[3,2,128,6144,1]{3,2,1,0,4:T(8,128)(2,1)} %bitcast.49), kind=kOutput, calls=%fused_computation.121 | convolution fusion | flops 4831838208 | bytes 17301504 | tf_op jit(solution)/shard_map/dot_general | solution.py:44
  279.3 0.0 copy-start.3
  279.3 0.0 copy-start.4
  279.3 0.1 slice_reduce_fusion.1
  279.4 0.1 multiply_reduce_fusion.1
  279.6 0.4 copy-done.3
  280.0 0.0 copy-done.4
  280.0 0.4 fusion.15
  280.4 0.3 fusion.16
  280.7 0.2 copy.21
  280.9 181.7 %all-gather.14.cloned.1.call-done = bf16[768,6144]{1,0:T(8,128)(2,1)} async-done(((bf16[768,768]{1,0:T(8,128)(2,1)}), bf16[768,6144]{1,0:T(8,128)(2,1)}) %all-gather.14.cloned.1.call-update) | async-done | bytes 9437200 | tf_op jit(solution)/shard_map/all_gather | solution.py:61
  462.6 192.6 %all-gather.12.cloned.1.call-done = bf16[6144,768]{1,0:T(8,128)(2,1)} async-done(((bf16[768,768]{1,0:T(8,128)(2,1)}), bf16[6144,768]{1,0:T(8,128)(2,1)}) %all-gather.12.cloned.1.call-update) | async-done | bytes 9437200 | tf_op jit(solution)/shard_map/all_gather | solution.py:48
  655.2 26.3 %fusion.17 = f32[512,6144]{1,0:T(8,128)} fusion(bf16[768,6144]{1,0:T(8,128)(2,1)} %all-gather.14.cloned.1.call-done, bf16[512,6144]{1,0:T(8,128)(2,1)} %fusion.4, bf16[6144,768]{1,0:T(8,128)(2,1)} %all-gather.12.cloned.1.call-done), kind=kOutput, calls=%fused_computation.32 | convolution fusion | flops 9689235456 | bytes 37748736 | tf_op jit(solution)/shard_map/dot_general | solution.py:59
  681.5 48.4 %all-gather.10.cloned.1.call-done = bf16[256,6144]{1,0:T(8,128)(2,1)} async-done(((bf16[256,768]{1,0:T(8,128)(2,1)}), bf16[256,6144]{1,0:T(8,128)(2,1)}) %all-gather.10.cloned.1.call-update) | async-done | bytes 3145744 | tf_op jit(solution)/shard_map/all_gather | solution.py:56
  729.9 9.9 %add_convert_fusion = bf16[512,6144]{1,0:T(8,128)(2,1)} fusion(f32[512,6144]{1,0:T(8,128)} %fusion.17, bf16[256,6144]{1,0:T(8,128)(2,1)} %all-gather.10.cloned.1.call-done, bf16[64,8,2,128]{3,2,1,0:T(2,128)(2,1)S(1)} %bitcast.47), kind=kOutput, calls=%fused_computation.7 | convolution fusion | flops 1616904192 | bytes 22282240 | tf_op jit(solution)/shard_map/dot_general | solution.py:54
  739.8 8.7 %copy.26 = bf16[512,6144]{0,1:T(8,128)(2,1)} copy(bf16[512,6144]{1,0:T(8,128)(2,1)} %add_convert_fusion) | data formatting | bytes 12582912
  748.5 0.0 copy-start.1
  748.5 0.0 reduce-scatter.4.cloned.1.call-update
  748.5 90.9 %reduce-scatter.4.cloned.1.call-done = bf16[384,512]{1,0:T(8,128)(2,1)} async-done(((bf16[6144,512]{1,0:T(8,128)(2,1)}), bf16[384,512]{1,0:T(8,128)(2,1)}) %reduce-scatter.4.cloned.1.call-update) | async-done | bytes 393232
  839.4 1.2 copy.27
  840.6 0.0 copy-done.1
  840.7 0.8 add_convert_fusion.1
  (5 shorter events, 0.0 us)
Async XLA Ops:
  6.5 75.1 %all-gather.6.cloned.1.call-start = ((), (), s32[]{:S(2)}) async-start(), calls=%async_computation.1 | async-start | bytes 6684672 | tf_op jit(solution)/shard_map/all_gather | solution.py:39
  7.3 262.5 %all-gather.8.cloned.1.call-start = ((), (), s32[]{:S(2)}) async-start(), calls=%async_computation.2 | async-start | bytes 10616832 | tf_op jit(solution)/shard_map/all_gather | solution.py:47
  9.7 452.8 %all-gather.14.cloned.1.call-start = ((), (), s32[]{:S(2)}) async-start(), calls=%async_computation.5 | async-start | bytes 10616832 | tf_op jit(solution)/shard_map/all_gather | solution.py:61
  10.5 644.7 %all-gather.12.cloned.1.call-start = ((), (), s32[]{:S(2)}) async-start(), calls=%async_computation.4 | async-start | bytes 10616832 | tf_op jit(solution)/shard_map/all_gather | solution.py:48
  11.0 718.9 %all-gather.10.cloned.1.call-start = ((), (), s32[]{:S(2)}) async-start(), calls=%async_computation.3 | async-start | bytes 3538944 | tf_op jit(solution)/shard_map/all_gather | solution.py:56
  11.6 827.8 %reduce-scatter.4.cloned.1.call-start = ((), (), s32[]{:S(2)}) async-start(), calls=%async_computation.6 | async-start | bytes 6684672
  81.6 4.6 copy-start
  86.2 1.8 copy-start.2
  279.3 0.7 copy-start.3
  279.3 0.7 copy-start.4
  748.5 92.1 %copy-start.1 = (bf16[512,384]{1,0:T(8,128)(2,1)S(1)}, bf16[512,384]{1,0:T(8,128)(2,1)}, u32[]{:S(2)}) copy-start(bf16[512,384]{1,0:T(8,128)(2,1)} %param.8) | copy-start | bytes 1179652
Sparse Core Ops, SparseCore 0:
  9.6 71.9 all-gather.5
  83.3 186.4 all-gather.7
  271.4 191.0 all-gather.13
  464.1 191.0 all-gather.11
  656.7 73.1 all-gather.9
  748.7 90.7 reduce-scatter.3
where the time goes:
time: 849 us; the launch traced here: 848 us
  waiting for transfers between devices  761 us (90%)
  matrix products  46.5 us (5%)
  local copies, waits for them, and re-layouts  13.6 us (2%)
  between operations  13.6 us (2%)
  other arithmetic  13 us (2%)
    all_gather x1, waiting for transfers between devices, shards(): lax.all_gather(w_up, 'row', axis=0, tiled=True)  193 us
    all_gather x1, waiting for transfers between devices, shards(): lax.all_gather(w_down, 'row', axis=1, tiled=True)  182 us
    all_gather x1, waiting for transfers between devices, shards(): lax.all_gather(w_qkv, 'row', axis=0, tiled=True)  175 us
    unnamed x7, waiting for transfers between devices  93.4 us
    all_gather x1, waiting for transfers between devices, shards(): gathered = lax.all_gather(tokens, 'col', axis=1, tiled=True)  70 us
    all_gather x1, waiting for transfers between devices, shards(): lax.all_gather(w_out, 'row', axis=1, tiled=True)  48.4 us
    dot_general x1, matrix products, shards(): jnp.dot(activated, lax.all_gather(w_down, 'row', axis=1, tiled=True), pre...  26.3 us
  transfers between devices with their start and end apart: 6, of which 6 were waited for; matrix products, arithmetic and copies ran while one was open for 6% of the time, Pallas kernels for 0%

commit v1 on v0

--- a/solution.py
+++ b/solution.py
@@ -7,6 +7,13 @@
 HD = 128
 PATCHES = 256
 epsilon = 1e-06
+
+
+def exchange_gather(x, name, d):
+    size = lax.axis_size(name)
+    blocks = jnp.stack([x for _ in range(size)])
+    blocks = lax.all_to_all(blocks, name, split_axis=0, concat_axis=0)
+    return jnp.concatenate(blocks, axis=d)
 
 
 def layer_norm(values_in, gain_vec):
@@ -57,9 +64,7 @@
         preferred_element_type=jnp.float32,
     )
     column_block = column_block + jnp.dot(
-        activated,
-        lax.all_gather(w_down, "row", axis=1, tiled=True),
-        preferred_element_type=jnp.float32,
+        activated, exchange_gather(w_down, "row", 1), preferred_element_type=jnp.float32
     )
     summed = lax.psum_scatter(
         column_block.astype(jnp.bfloat16), "col", scatter_dimension=1, tiled=True

time: 849 us -> 738 us (0.87)
  waiting for transfers between devices: 761 us -> 640 us
    all_gather x1 -> x0, waiting for transfers between devices: 182 us -> none  [shards(): lax.all_gather(w_down, 'row', axis=1, tiled=True)]
    all_gather x1, waiting for transfers between devices: 70 us -> 142 us  [shards(): gathered = lax.all_gather(tokens, 'col', axis=1, tiled=True)]
    all_gather x1, waiting for transfers between devices: 193 us -> 182 us  [shards(): lax.all_gather(w_up, 'row', axis=0, tiled=True)]
    unnamed x7 -> x6, waiting for transfers between devices: 93.4 us -> 92.8 us
  transfers between devices with their start and end apart: 6 -> 6, of which waited for: 6 -> 5; matrix products, arithmetic and copies ran while one was open for 6% -> 8% of each run, Pallas kernels for 0% -> 0%
where the time goes in v1:
time: 738 us
  waiting for transfers between devices  640 us (87%)
  matrix products  46.5 us (6%)
  local copies, waits for them, and re-layouts  18.9 us (3%)
  between operations  13.2 us (2%)
  other arithmetic  13 us (2%)
    all_gather x1, waiting for transfers between devices, shards(): lax.all_gather(w_up, 'row', axis=0, tiled=True)  182 us
    all_gather x1, waiting for transfers between devices, shards(): lax.all_gather(w_qkv, 'row', axis=0, tiled=True)  175 us
    all_gather x1, waiting for transfers between devices, shards(): gathered = lax.all_gather(tokens, 'col', axis=1, tiled=True)  142 us
    unnamed x6, waiting for transfers between devices  92.8 us
    all_gather x1, waiting for transfers between devices, shards(): lax.all_gather(w_out, 'row', axis=1, tiled=True)  48.5 us
    dot_general x1, matrix products, shards(): jnp.dot(activated, exchange_gather(w_down, 'row', 1), preferred_element_t...  26.2 us
  transfers between devices with their start and end apart: 6, of which 5 were waited for; matrix products, arithmetic and copies ran while one was open for 8% of the time, Pallas kernels for 0%

profile of v1, /device:TPU:0, one launch (start us, length us, event | category | flops | bytes accessed | tf_op | source)
XLA Modules:
  0.0 737.9 jit_solution(1862557681402801996)
XLA Ops:
  6.5 0.0 all-gather.5.cloned.1.call-start
  6.5 0.7 all-gather.5.cloned.1.call-update
  7.3 0.0 all-gather.7.cloned.1.call-start
  7.3 2.4 copy.18
  9.7 0.0 copy-start.2
  9.7 0.0 all-gather.7.cloned.1.call-update
  9.7 0.0 all-gather.11.cloned.1.call-start
  9.8 0.7 all-gather.11.cloned.1.call-update
  10.5 0.5 copy-done.2
  11.0 0.6 copy.23
  11.6 4.1 stack.2
  15.7 5.9 all-to-all-start
  21.6 0.0 all-gather.9.cloned.1.call-start
  21.7 0.5 all-gather.9.cloned.1.call-update
  22.2 0.0 reduce-scatter.4.cloned.1.call-start
  22.3 142.0 %all-gather.5.cloned.1.call-done = bf16[512,6144]{1,0:T(8,128)(2,1)} async-done(((bf16[512,384]{1,0:T(8,128)(2,1)}), bf16[512,6144]{1,0:T(8,128)(2,1)}) %all-gather.5.cloned.1.call-update) | async-done | bytes 6291472 | tf_op jit(solution)/shard_map/all_gather | solution.py:46
  164.3 0.0 copy-start
  164.3 3.8 convert_reduce_fusion
  168.1 0.7 copy-done
  168.9 0.0 copy-start.3
  168.9 1.8 fusion.2
  170.7 0.0 copy-done.3
  170.7 6.3 fusion.4
  177.0 175.2 %all-gather.7.cloned.1.call-done = bf16[6144,3,256]{0,2,1:T(8,128)(2,1)} async-done(((bf16[768,3,256]{0,2,1:T(8,128)(2,1)}), bf16[6144,3,256]{0,2,1:T(8,128)(2,1)}) %all-gather.7.cloned.1.call-update) | async-done | bytes 9437200 | tf_op jit(solution)/shard_map/all_gather | solution.py:54
  352.1 9.5 %fusion.93 = f32[2,256,3,2,128]{1,4,3,2,0:T(8,128)S(1)} fusion(bf16[2,256,6144,1,1]{2,1,4,3,0:T(8,128)(2,1)} %bitcast.49, bf16[3,2,128,6144,1]{3,2,1,0,4:T(8,128)(2,1)} %bitcast.52), kind=kOutput, calls=%fused_computation.121 | convolution fusion | flops 4831838208 | bytes 17301504 | tf_op jit(solution)/shard_map/dot_general | solution.py:51
  361.7 0.0 copy-start.4
  361.7 0.0 copy-start.5
  361.7 0.1 slice_reduce_fusion.1
  361.8 0.1 multiply_reduce_fusion.1
  362.0 0.4 copy-done.4
  362.3 0.0 copy-done.5
  362.3 0.4 fusion.15
  362.8 0.3 fusion.16
  363.1 0.2 copy.22
  363.3 0.0 all-to-all-done
  363.3 181.6 %all-gather.11.cloned.1.call-done = bf16[6144,768]{1,0:T(8,128)(2,1)} async-done(((bf16[768,768]{1,0:T(8,128)(2,1)}), bf16[6144,768]{1,0:T(8,128)(2,1)}) %all-gather.11.cloned.1.call-update) | async-done | bytes 9437200 | tf_op jit(solution)/shard_map/all_gather | solution.py:55
  544.9 26.2 %fusion.17 = f32[512,6144]{1,0:T(8,128)} fusion(bf16[768,6144]{0,1:T(8,128)(2,1)} %bitcast.12, bf16[512,6144]{1,0:T(8,128)(2,1)} %fusion.4, bf16[6144,768]{1,0:T(8,128)(2,1)} %all-gather.11.cloned.1.call-done), kind=kOutput, calls=%fused_computation.32 | convolution fusion | flops 9689235456 | bytes 37748736 | tf_op jit(solution)/shard_map/dot_general | solution.py:66
  571.2 48.5 %all-gather.9.cloned.1.call-done = bf16[256,6144]{1,0:T(8,128)(2,1)} async-done(((bf16[256,768]{1,0:T(8,128)(2,1)}), bf16[256,6144]{1,0:T(8,128)(2,1)}) %all-gather.9.cloned.1.call-update) | async-done | bytes 3145744 | tf_op jit(solution)/shard_map/all_gather | solution.py:63
  619.6 10.0 %add_convert_fusion = bf16[512,6144]{1,0:T(8,128)(2,1)} fusion(f32[512,6144]{1,0:T(8,128)} %fusion.17, bf16[256,6144]{1,0:T(8,128)(2,1)} %all-gather.9.cloned.1.call-done, bf16[64,8,2,128]{3,2,1,0:T(2,128)(2,1)S(1)} %bitcast.50), kind=kOutput, calls=%fused_computation.7 | convolution fusion | flops 1616904192 | bytes 22282240 | tf_op jit(solution)/shard_map/dot_general | solution.py:61
  629.7 8.7 %copy.28 = bf16[512,6144]{0,1:T(8,128)(2,1)} copy(bf16[512,6144]{1,0:T(8,128)(2,1)} %add_convert_fusion) | data formatting | bytes 12582912
  638.4 0.0 copy-start.1
  638.4 0.0 reduce-scatter.4.cloned.1.call-update
  638.4 90.9 %reduce-scatter.4.cloned.1.call-done = bf16[384,512]{1,0:T(8,128)(2,1)} async-done(((bf16[6144,512]{1,0:T(8,128)(2,1)}), bf16[384,512]{1,0:T(8,128)(2,1)}) %reduce-scatter.4.cloned.1.call-update) | async-done | bytes 393232
  729.3 1.2 copy.29
  730.5 0.0 copy-done.1
  730.5 0.8 add_convert_fusion.1
  (5 shorter events, 0.0 us)
Async XLA Ops:
  6.5 157.7 %all-gather.5.cloned.1.call-start = ((), (), s32[]{:S(2)}) async-start(), calls=%async_computation.2 | async-start | bytes 6684672 | tf_op jit(solution)/shard_map/all_gather | solution.py:46
  7.3 344.9 %all-gather.7.cloned.1.call-start = ((), (), s32[]{:S(2)}) async-start(), calls=%async_computation.3 | async-start | bytes 10616832 | tf_op jit(solution)/shard_map/all_gather | solution.py:54
  9.7 1.3 copy-start.2
  9.7 535.2 %all-gather.11.cloned.1.call-start = ((), (), s32[]{:S(2)}) async-start(), calls=%async_computation.5 | async-start | bytes 10616832 | tf_op jit(solution)/shard_map/all_gather | solution.py:55
  15.7 347.6 %all-to-all-start = ((bf16[8,768,768]{1,2,0:T(8,128)(2,1)}), bf16[8,768,768]{1,2,0:T(8,128)(2,1)}, u32[]{:S(2)}, u32[]{:S(2)}) async-start(bf16[8,768,768]{1,2,0:T(8,128)(2,1)} %stack.2), calls=%async_computation | async-start | bytes 18874368 | tf_op jit(solution)/shard_map/all_to_all | solution.py:15
  21.6 598.0 %all-gather.9.cloned.1.call-start = ((), (), s32[]{:S(2)}) async-start(), calls=%async_computation.4 | async-start | bytes 3538944 | tf_op jit(solution)/shard_map/all_gather | solution.py:63
  22.2 707.1 %reduce-scatter.4.cloned.1.call-start = ((), (), s32[]{:S(2)}) async-start(), calls=%async_computation.6 | async-start | bytes 6684672
  164.3 4.6 copy-start
  168.9 1.8 copy-start.3
  361.7 0.7 copy-start.4
  361.7 0.7 copy-start.5
  638.4 92.1 %copy-start.1 = (bf16[512,384]{1,0:T(8,128)(2,1)S(1)}, bf16[512,384]{1,0:T(8,128)(2,1)}, u32[]{:S(2)}) copy-start(bf16[512,384]{1,0:T(8,128)(2,1)} %param.8) | copy-start | bytes 1179652
Sparse Core Ops, SparseCore 0:
  9.6 154.6 all-gather.4
  165.9 186.1 all-gather.6
  353.8 191.0 all-gather.10
  546.4 73.1 all-gather.8
  638.5 90.7 reduce-scatter.3
